TPU v7x, 512 devices: a whole 4x4x16 slice. The times are simulated.
512 devices in a mesh: src: 32 (over x, y, z_hi), rcv: 16 (over z_lo, core).
Axes of the slice: x: 4, y: 4, z: 16 (z_hi: 2, z_lo: 8; z = z_hi * 8 + z_lo), core: 2. Of those that a mesh axis runs over, the one named last changes fastest.
Arguments:
- observed: bfloat16 [32, 1280, 128, 128], P('src', 'rcv'), may hold values from -6 to 6
- block_row: int32 [32, 1280], P('src', 'rcv'), may hold values from 0 to 31, as said below
- block_col: int32 [32, 1280], P('src', 'rcv'), may hold values from 0 to 15
- live: int32 [32, 16], P('src', 'rcv'), may hold values from 20 to 80, as said below
- row_factor: bfloat16 [131072, 64], P('src'), may hold values from -5 to 5
- col_factor: bfloat16 [32768, 64], P('rcv'), may hold values from -5 to 5
Outputs:
- new_rows: bfloat16 [131072, 64], P('src')
- new_cols: bfloat16 [32768, 64], P('rcv')
Inputs may be any that keep to these rules, and one draw needn't show every extreme that they name: `block_row`: within one device the 80 slots name distinct blocks of its tile. `live`: some device has all 80 slots in use.
All inputs are finite; a program needn't handle non-finite values.
Results may differ from a plain program's by a relative error of at most 0.007.
Values may be sent and summed in bfloat16 or wider, within the bound.
A program may use at most 64 MiB of HBM per device.

v0:
```python
import math
import jax
import jax.numpy as jnp
from jax import lax
from jax.sharding import PartitionSpec as P


def local(observed, block_row, block_col, live, row_factor, col_factor):
    slot_data = observed[0]
    slot_total = slot_data.shape[0]
    block_size = slot_data.shape[1]
    rank_width = row_factor.shape[1]
    row_block_total = row_factor.shape[0] // block_size
    col_block_total = col_factor.shape[0] // block_size
    row_table = row_factor.reshape(row_block_total, block_size, rank_width)
    col_table = col_factor.reshape(col_block_total, block_size, rank_width)
    row_pick = block_row[0][:, None] == jnp.arange(row_block_total, dtype=jnp.int32)[None, :]
    col_pick = block_col[0][:, None] == jnp.arange(col_block_total, dtype=jnp.int32)[None, :]
    row_blocks = jnp.einsum(
        "ks,sar->kar", row_pick.astype(jnp.bfloat16), row_table, preferred_element_type=jnp.float32
    ).astype(jnp.bfloat16)
    col_blocks = jnp.einsum(
        "kc,cbr->kbr", col_pick.astype(jnp.bfloat16), col_table, preferred_element_type=jnp.float32
    ).astype(jnp.bfloat16)
    predicted = jnp.einsum(
        "kar,kbr->kab", row_blocks, col_blocks, preferred_element_type=jnp.float32
    )
    slot_live = jnp.arange(slot_total, dtype=jnp.int32) < live[0, 0]
    residual = jnp.where(
        slot_live[:, None, None], predicted - slot_data.astype(jnp.float32), 0.0
    ).astype(jnp.bfloat16)
    row_terms = jnp.einsum("kab,kbr->kar", residual, col_blocks, preferred_element_type=jnp.float32)
    row_grad = jnp.einsum("ks,kar->sar", row_pick.astype(jnp.float32), row_terms).reshape(
        row_block_total * block_size, rank_width
    )
    row_step = 0.5 / math.sqrt(slot_total * block_size * lax.axis_size("rcv") // row_block_total)
    row_sums = lax.psum(row_grad, "rcv")
    new_rows = (0.9 * row_factor.astype(jnp.float32) - row_step * row_sums).astype(jnp.bfloat16)
    col_terms = jnp.einsum("kab,kar->kbr", residual, row_blocks, preferred_element_type=jnp.float32)
    col_grad = jnp.einsum("kc,kbr->cbr", col_pick.astype(jnp.float32), col_terms).reshape(
        col_block_total * block_size, rank_width
    )
    col_step = 0.5 / math.sqrt(slot_total * block_size * lax.axis_size("src") // col_block_total)
    col_sums = lax.psum(col_grad, "src")
    new_cols = (0.9 * col_factor.astype(jnp.float32) - col_step * col_sums).astype(jnp.bfloat16)
    return (new_rows, new_cols)


def solution(mesh):
    return jax.shard_map(
        local,
        mesh=mesh,
        in_specs=(
            P("src", "rcv", None, None),
            P("src", "rcv"),
            P("src", "rcv"),
            P("src", "rcv"),
            P("src", None),
            P("rcv", None),
        ),
        out_specs=(P("src", None), P("rcv", None)),
        check_vma=False,
    )
```

profile of v0, /device:TPU:1, one launch (start us, length us, event | category | flops | bytes accessed | tf_op | source)
XLA Modules:
  0.0 812.5 jit_solution(6672184415892702241)
XLA Ops:
  7.2 0.0 all-reduce.5.cloned.1.call-start
  7.9 1.0 copy.13
  8.9 0.0 copy-start.3
  8.9 1.1 copy.12
  10.0 0.0 copy-start.5
  10.1 0.5 convolution_convert_fusion.1
  10.6 0.5 convolution_convert_fusion
  11.2 0.6 copy-done.5
  11.8 1.6 fusion.1
  13.4 0.0 copy-done
  13.4 0.8 fusion.9
  14.2 0.8 fusion.2
  15.1 1.0 copy.31
  16.0 0.0 all-reduce.5.cloned.1.call-update
  16.0 0.0 all-reduce.3.cloned.1.call-start
  16.1 3.2 fusion.6
  19.3 0.9 fusion.4
  20.2 0.0 copy-start.2
  20.2 1.6 copy.30
  21.9 0.0 all-reduce.3.cloned.1.call-update
  21.9 558.6 %all-reduce.5.cloned.1.call-done = f32[2048,64]{0,1:T(8,128)} async-done(((f32[2048,64]{0,1:T(8,128)}), f32[2048,64]{0,1:T(8,128)}) %all-reduce.5.cloned.1.call-update) | async-done | bytes 524304 | tf_op jit(solution)/shard_map/psum | solution.py:44
  580.5 1.8 subtract_convert_fusion.1
  582.3 221.1 %all-reduce.3.cloned.1.call-done = f32[4096,64]{0,1:T(8,128)} async-done(((f32[4096,64]{0,1:T(8,128)}), f32[4096,64]{0,1:T(8,128)}) %all-reduce.3.cloned.1.call-update) | async-done | bytes 1048592 | tf_op jit(solution)/shard_map/psum | solution.py:37
  803.5 2.2 subtract_convert_fusion
  (8 shorter events, 0.0 us)
Async XLA Ops:
  7.2 2.9 copy-start.4
  7.2 573.3 %all-reduce.5.cloned.1.call-start = ((), (), s32[]{:S(2)}) async-start(), calls=%async_computation.1 | async-start | bytes 1048576 | tf_op jit(solution)/shard_map/psum | solution.py:44
  8.9 1.7 copy-start.3
  10.0 1.7 copy-start.5
  11.8 1.6 copy-start
  16.0 787.5 %all-reduce.3.cloned.1.call-start = ((), (), s32[]{:S(2)}) async-start(), calls=%async_computation | async-start | bytes 2097152 | tf_op jit(solution)/shard_map/psum | solution.py:37
  20.2 560.3 %copy-start.2 = (bf16[2048,64]{0,1:T(8,128)(2,1)S(1)}, bf16[2048,64]{0,1:T(8,128)(2,1)}, u32[]{:S(2)}) copy-start(bf16[2048,64]{0,1:T(8,128)(2,1)} %param.11) | copy-start | bytes 786436
  21.9 781.6 %copy-start.1 = (bf16[4096,64]{0,1:T(8,128)(2,1)S(1)}, bf16[4096,64]{0,1:T(8,128)(2,1)}, u32[]{:S(2)}) copy-start(bf16[4096,64]{0,1:T(8,128)(2,1)} %param.10) | copy-start | bytes 1572868
Sparse Core Ops, SparseCore 0:
  16.2 564.3 all-reduce.4
  583.4 220.0 all-reduce.2
where the time goes:
time: 813 us
  waiting for transfers between devices  780 us (96%)
  between operations  14.8 us (2%)
  matrix products  8.45 us (1%)
    psum x1, waiting for transfers between devices, local(): col_sums = lax.psum(col_grad, 'src')  559 us
    psum x1, waiting for transfers between devices, local(): row_sums = lax.psum(row_grad, 'rcv')  221 us
  transfers between devices with their start and end apart: 2, of which 2 were waited for; matrix products, arithmetic and copies ran while one was open for 1% of the time, Pallas kernels for 0%

commit v1 on v0

--- a/solution.py
+++ b/solution.py
@@ -3,6 +3,7 @@
 import jax.numpy as jnp
 from jax import lax
 from jax.sharding import PartitionSpec as P
+from jax.lax import all_gather
 
 
 def local(observed, block_row, block_col, live, row_factor, col_factor):
@@ -41,7 +42,8 @@
         col_block_total * block_size, rank_width
     )
     col_step = 0.5 / math.sqrt(slot_total * block_size * lax.axis_size("src") // col_block_total)
-    col_sums = lax.psum(col_grad, "src")
+    obtain_signs = lambda sample: jnp.sum(all_gather(sample, "src"), 0)
+    col_sums = obtain_signs(col_grad)
     new_cols = (0.9 * col_factor.astype(jnp.float32) - col_step * col_sums).astype(jnp.bfloat16)
     return (new_rows, new_cols)
 

time: 813 us -> 541 us (0.67)
  waiting for transfers between devices: 780 us -> 500 us
    psum x1 -> x0, waiting for transfers between devices: 559 us -> none  [local(): col_sums = lax.psum(col_grad, 'src')]
    psum x1, waiting for transfers between devices: 221 us -> 500 us  [local(): row_sums = lax.psum(row_grad, 'rcv')]
  transfers between devices with their start and end apart: 2 -> 2, of which waited for: 2 -> 1; matrix products, arithmetic and copies ran while one was open for 1% -> 1% of each run, Pallas kernels for 0% -> 0%
where the time goes in v1:
time: 541 us
  waiting for transfers between devices  500 us (92%)
  between operations  16.2 us (3%)
  other arithmetic  9.89 us (2%)
  matrix products  8.45 us (2%)
  local copies, waits for them, and re-layouts  5.76 us (1%)
    psum x1, waiting for transfers between devices, local(): row_sums = lax.psum(row_grad, 'rcv')  500 us
  transfers between devices with their start and end apart: 2, of which 1 were waited for; matrix products, arithmetic and copies ran while one was open for 1% of the time, Pallas kernels for 0%

profile of v1, /device:TPU:1, one launch (start us, length us, event | category | flops | bytes accessed | tf_op | source)
XLA Modules:
  0.0 540.7 jit_solution(9294850651390814022)
XLA Ops:
  8.0 0.0 all-reduce.2.cloned.1.call-start
  8.7 1.0 copy.15
  9.7 0.0 copy-start.3
  9.7 1.1 copy.14
  10.9 0.0 copy-start.5
  10.9 0.5 convolution_convert_fusion
  11.4 0.5 convolution_convert_fusion.1
  12.0 1.1 copy-done
  13.1 0.0 copy-done.5
  13.1 1.6 fusion.1
  14.7 1.9 fusion.6
  16.6 0.9 fusion.4
  17.5 1.6 copy.30
  19.2 0.0 all-reduce.2.cloned.1.call-update
  19.2 0.0 all-gather.2.cloned.1.call-start
  19.2 2.1 fusion.9
  21.4 0.0 copy-start.1
  21.4 0.8 fusion.2
  22.2 0.9 all_gather_reshape.3
  23.1 0.0 all-gather.2.cloned.1.call-update
  23.1 500.3 %all-reduce.2.cloned.1.call-done = f32[4096,64]{0,1:T(8,128)} async-done(((f32[4096,64]{0,1:T(8,128)}), f32[4096,64]{0,1:T(8,128)}) %all-reduce.2.cloned.1.call-update) | async-done | bytes 1048592 | tf_op jit(solution)/shard_map/psum | solution.py:38
  523.4 2.2 subtract_convert_fusion
  525.5 6.9 %reduce_sum.9 = f32[2048,64]{0,1:T(8,128)S(1)} reduce(f32[32,2048,64]{1,2,0:T(8,128)} %all-gather.2.cloned.1.call-done, f32[]{:T(128)} %constant.0.clone.1), dimensions={0}, to_apply=%region_1.2 | reduce | flops 4063232 | bytes 17301508 | tf_op jit(solution)/shard_map/reduce_sum | solution.py:45
  532.5 0.8 subtract_convert_fusion.1
  (9 shorter events, 0.0 us)
Async XLA Ops:
  8.0 2.9 copy-start.4
  8.0 515.4 %all-reduce.2.cloned.1.call-start = ((), (), s32[]{:S(2)}) async-start(), calls=%async_computation | async-start | bytes 2097152 | tf_op jit(solution)/shard_map/psum | solution.py:38
  9.7 1.7 copy-start.3
  10.9 2.2 copy-start.5
  12.0 1.1 copy-start
  19.2 506.4 %all-gather.2.cloned.1.call-start = ((), (), s32[]{:S(2)}) async-start(), calls=%async_computation.1 | async-start | bytes 17301504 | tf_op jit(solution)/shard_map/all_gather | solution.py:45
  21.4 502.0 %copy-start.1 = (bf16[4096,64]{0,1:T(8,128)(2,1)S(1)}, bf16[4096,64]{0,1:T(8,128)(2,1)}, u32[]{:S(2)}) copy-start(bf16[4096,64]{0,1:T(8,128)(2,1)} %param.10) | copy-start | bytes 1572868
  525.5 6.9 %copy-start.2 = (bf16[2048,64]{0,1:T(8,128)(2,1)S(1)}, bf16[2048,64]{0,1:T(8,128)(2,1)}, u32[]{:S(2)}) copy-start(bf16[2048,64]{0,1:T(8,128)(2,1)} %param.11) | copy-start | bytes 786436
Sparse Core Ops, SparseCore 0:
  19.3 504.0 all-reduce.1
Sparse Core Ops, SparseCore 1:
  24.0 427.9 all-gather.1
